TPU v7x, 256 devices: a whole 4x4x8 slice. The times are simulated.
256 devices in a mesh: role: 2 (over z_hi), dp: 32 (over x, z_lo, core), mp: 4 (over y).
Axes of the slice: x: 4, y: 4, z: 8 (z_hi: 2, z_lo: 4; z = z_hi * 4 + z_lo), core: 2. Of those that a mesh axis runs over, the one named last changes fastest.
Arguments:
- state: float32 [2, 2, 8, 2048, 512], P('role', None, None, 'dp', 'mp'), may hold values from 0 to 1
- embed: bfloat16 [2, 1024, 4096], P('role', 'dp', 'mp'), may hold values from -0.09375 to 0.09375
- mlp: bfloat16 [2, 2, 1024, 4096], P('role', None, 'dp', 'mp'), may hold values from -0.1875 to 0.1875
- mom_embed: float32 [2, 1024, 4096], P('role', 'dp', 'mp'), may hold values from -6 to 6
- mom_mlp: float32 [2, 2, 1024, 4096], P('role', None, 'dp', 'mp'), may hold values from -6 to 6
Outputs:
- state_out: float32 [2, 8, 2048, 512], P(None, None, 'dp', 'mp')
- embed_out: bfloat16 [2, 1024, 4096], P('role', 'dp', 'mp')
- mlp_out: bfloat16 [2, 2, 1024, 4096], P('role', None, 'dp', 'mp')
- mom_embed_out: float32 [2, 1024, 4096], P('role', 'dp', 'mp')
- mom_mlp_out: float32 [2, 2, 1024, 4096], P('role', None, 'dp', 'mp')
All inputs are finite; a program needn't handle non-finite values.
Results may differ from a plain program's by a relative error of at most 0.0034.
Values may be sent and summed in bfloat16 or wider, within the bound.
A program may use at most 128 MiB of HBM per device.

v0:
```python
import jax
import jax.numpy as jnp
from jax import lax
from jax.sharding import PartitionSpec as P

PATCH = 16
STEPS = 4
SUBSTRATE_DIFFUSION = 0.2
CATALYST_DIFFUSION = 0.1
FEED_RATE = 0.037
KILL_RATE = 0.06
TIME_STEP = 0.8
GELU_FACTOR = 0.7978845608028654
MOMENTUM_DECAY = 0.9
LEARNING_RATE = 0.003


def extended(cells, sides, width):
    for axis, dim in sides:
        count = lax.axis_size(axis)
        head = lax.slice_in_dim(cells, 0, width, axis=dim)
        tail = lax.slice_in_dim(cells, cells.shape[dim] - width, cells.shape[dim], axis=dim)
        cells = jnp.concatenate(
            [
                lax.ppermute(tail, axis, [(i, (i + 1) % count) for i in range(count)]),
                cells,
                lax.ppermute(head, axis, [((i + 1) % count, i) for i in range(count)]),
            ],
            axis=dim,
        )
    return cells


def from_behind(value, axis, steps):
    count = lax.axis_size(axis)
    leading, last = (max(0, -steps), min(count, count - steps))
    return lax.ppermute(value, axis, [(source, source + steps) for source in range(leading, last)])


def in_blocks(x, dim, count):
    before, after = (x.shape[:dim], x.shape[dim + 1 :])
    return jnp.moveaxis(x.reshape(*before, count, -1, *after), dim, 0)


def summed_on_arrival(x, axis, dim):
    count = lax.axis_size(axis)
    tiles = lax.all_to_all(in_blocks(x, dim, count), axis, 0, 0, tiled=True)
    return jnp.sum(tiles, axis=0)


def joined_along(tiles, dim):
    tiles = jnp.moveaxis(tiles, 0, dim)
    shape = tiles.shape
    return tiles.reshape(*shape[:dim], shape[dim] * shape[dim + 1], *shape[dim + 2 :])


def copy_for_each(x, axis):
    copies = jnp.broadcast_to(x, (lax.axis_size(axis), *x.shape))
    return lax.all_to_all(copies, axis, split_axis=0, concat_axis=0, tiled=True)


def gathered_copies(x, axis, dim):
    return joined_along(copy_for_each(x, axis), dim)


def react(padded):
    center = padded[:, :, 1:-1, 1:-1]
    below_plane = jnp.concatenate([center[:, :1], center[:, :-1]], axis=1)
    above_plane = jnp.concatenate([center[:, 1:], center[:, -1:]], axis=1)
    beside = below_plane + above_plane + padded[:, :, :-2, 1:-1] + padded[:, :, 2:, 1:-1]
    beside = beside + padded[:, :, 1:-1, :-2] + padded[:, :, 1:-1, 2:]
    laplace = beside - 6.0 * center
    substrate = center[0]
    catalyst = center[1]
    growth = substrate * catalyst * catalyst
    new_substrate = substrate + TIME_STEP * (
        SUBSTRATE_DIFFUSION * laplace[0] - growth + FEED_RATE * (1.0 - substrate)
    )
    new_catalyst = catalyst + TIME_STEP * (
        CATALYST_DIFFUSION * laplace[1] + growth - (FEED_RATE + KILL_RATE) * catalyst
    )
    return jnp.stack([new_substrate, new_catalyst])


def gelu_slope(preact):
    cubic = 0.044715 * preact * preact * preact
    tangent = jnp.tanh(GELU_FACTOR * (preact + cubic))
    return 0.5 * (1.0 + tangent) + 0.5 * preact * (1.0 - tangent * tangent) * GELU_FACTOR * (
        1.0 + 3.0 * 0.044715 * preact * preact
    )


def to_patches(brick):
    extent = brick.shape
    blocks = brick.reshape(
        extent[0], extent[1], extent[2] // PATCH, PATCH, extent[3] // PATCH, PATCH
    )
    blocks = blocks.transpose(2, 4, 0, 1, 3, 5)
    return blocks.reshape(
        extent[2] // PATCH * (extent[3] // PATCH), extent[0] * extent[1] * PATCH * PATCH
    )


def advance(cells):
    padded = extended(cells, (("dp", 2), ("mp", 3)), STEPS)
    for iteration in range(STEPS):
        padded = react(padded)
    return padded


def shards(state, embed, mlp, mom_embed, mom_mlp):
    group_index = lax.axis_index("role")
    start_cells = state[0]
    start_half = start_cells.astype(jnp.bfloat16)
    arranged = lax.all_to_all(to_patches(start_half), "mp", split_axis=1, concat_axis=0, tiled=True)
    initial_rows = from_behind(arranged, "role", 1)
    stacked = jnp.concatenate([embed[0], mlp[0, 0], mlp[0, 1]], axis=1)
    whole = lax.all_gather(stacked, "dp", axis=0, tiled=True)
    cells = advance(start_cells)
    arrived = from_behind(cells, "role", 1)
    state_out = jnp.where(group_index == 0, cells, arrived)
    final_rows = to_patches(arrived.astype(jnp.bfloat16))
    targets = lax.all_to_all(final_rows, "mp", split_axis=1, concat_axis=0, tiled=True)
    feature_cols = embed.shape[2]
    hidden_cols = mlp.shape[3]
    embed_full = whole[:, :feature_cols]
    up_full = whole[:, feature_cols : feature_cols + hidden_cols]
    down_full = whole[:, feature_cols + hidden_cols :]
    patch_rows = initial_rows.shape[0]
    loss_scale = float(patch_rows * lax.axis_size("dp")) ** (-0.5)
    embedded = summed_on_arrival(
        jnp.dot(initial_rows, embed_full.T, preferred_element_type=jnp.float32), "mp", 0
    )
    recip = lax.rsqrt(jnp.mean(embedded * embedded, axis=1, keepdims=True) + 1e-06)
    normed = gathered_copies((embedded * recip).astype(jnp.bfloat16), "mp", 0)
    hidden_pre = jnp.dot(normed, up_full, preferred_element_type=jnp.float32)
    active = jax.nn.gelu(hidden_pre, approximate=True).astype(jnp.bfloat16)
    branch = summed_on_arrival(
        jnp.dot(active, down_full.T, preferred_element_type=jnp.float32), "mp", 0
    )
    stream = gathered_copies((embedded + branch).astype(jnp.bfloat16), "mp", 0)
    predicted = initial_rows.astype(jnp.float32) + jnp.dot(
        stream, embed_full, preferred_element_type=jnp.float32
    )
    residual_grad = ((predicted - targets.astype(jnp.float32)) * loss_scale).astype(jnp.bfloat16)
    stream_grad = summed_on_arrival(
        jnp.dot(residual_grad, embed_full.T, preferred_element_type=jnp.float32), "mp", 0
    )
    stream_sent = gathered_copies(stream_grad.astype(jnp.bfloat16), "mp", 0)
    hidden_grad = (
        jnp.dot(stream_sent, down_full, preferred_element_type=jnp.float32) * gelu_slope(hidden_pre)
    ).astype(jnp.bfloat16)
    normed_grad = summed_on_arrival(
        jnp.dot(hidden_grad, up_full.T, preferred_element_type=jnp.float32), "mp", 0
    )
    embed_grad = (
        stream_grad
        + recip * normed_grad
        - embedded
        * (recip * recip * recip)
        * jnp.mean(normed_grad * embedded, axis=1, keepdims=True)
    )
    embed_sent = gathered_copies(embed_grad.astype(jnp.bfloat16), "mp", 0)
    up_part = jnp.dot(normed.T, hidden_grad, preferred_element_type=jnp.float32)
    down_part = jnp.dot(stream_sent.T, active, preferred_element_type=jnp.float32)
    first = jnp.dot(stream.T, residual_grad, preferred_element_type=jnp.float32)
    grads = lax.psum_scatter(
        jnp.concatenate(
            [
                first + jnp.dot(embed_sent.T, initial_rows, preferred_element_type=jnp.float32),
                up_part,
                down_part,
            ],
            axis=1,
        ),
        "dp",
        scatter_dimension=0,
        tiled=True,
    )
    mirrored = from_behind(grads, "role", -1)
    grads = jnp.where(group_index == 0, mirrored, grads)
    grad_embed_rows = grads[:, :feature_cols]
    grad_mlp_rows = jnp.stack(
        [
            grads[:, feature_cols : feature_cols + hidden_cols],
            grads[:, feature_cols + hidden_cols :],
        ]
    )
    mom_embed_out = MOMENTUM_DECAY * mom_embed + grad_embed_rows[None]
    mom_mlp_out = MOMENTUM_DECAY * mom_mlp + grad_mlp_rows[None]
    embed_out = (embed.astype(jnp.float32) - LEARNING_RATE * mom_embed_out).astype(jnp.bfloat16)
    mlp_out = (mlp.astype(jnp.float32) - LEARNING_RATE * mom_mlp_out).astype(jnp.bfloat16)
    return (state_out, embed_out, mlp_out, mom_embed_out, mom_mlp_out)


def solution(mesh):
    placed = (
        P("role", None, None, "dp", "mp"),
        P("role", "dp", "mp"),
        P("role", None, "dp", "mp"),
        P("role", "dp", "mp"),
        P("role", None, "dp", "mp"),
    )
    return jax.shard_map(
        shards,
        mesh=mesh,
        in_specs=placed,
        out_specs=(
            P(None, None, "dp", "mp"),
            P("role", "dp", "mp"),
            P("role", None, "dp", "mp"),
            P("role", "dp", "mp"),
            P("role", None, "dp", "mp"),
        ),
        check_vma=False,
    )
```

profile of v0, /device:TPU:24, one launch (start us, length us, event | category | flops | bytes accessed | tf_op | source)
XLA Modules:
  0.0 440.8 jit_solution(15371048117641775478)
XLA Ops:
  8.2 1.5 pad_maximum_fusion.6
  10.1 6.3 %collective-permute-start.1 = (f32[2,8,4,128]{3,1,2,0:T(8,128)S(1)}, f32[2,8,4,128]{3,1,2,0:T(8,128)S(1)}, u32[]{:S(2)}, u32[]{:S(2)}) collective-permute-start(f32[2,8,4,128]{3,1,2,0:T(8,128)S(1)} %get-tuple-element.66), channel_id=1, source_target_pairs={{4,0},{8,4},{12,8},{16,12},{20,16},{24,20},{28,24},{32,28},{36,32}... | collective-permute-start | bytes 98312 | tf_op jit(solution)/shard_map/ppermute | solution.py:27
  16.4 1.6 collective-permute-done.1
  18.0 5.6 %collective-permute-done = f32[2,8,4,128]{3,1,2,0:T(8,128)S(1)} collective-permute-done((f32[2,8,4,128]{3,1,2,0:T(8,128)S(1)}, f32[2,8,4,128]{3,1,2,0:T(8,128)S(1)}, u32[]{:S(2)}, u32[]{:S(2)}) %collective-permute-start) | collective-permute-done | bytes 32800 | tf_op jit(solution)/shard_map/ppermute | solution.py:25
  25.2 2.5 collective-permute-start.2
  27.8 1.4 convert_element_type.57
  29.1 1.9 copy.104
  31.1 3.8 all_to_all.48
  35.6 4.5 %all-to-all-start = ((bf16[32,4,1024]{2,0,1:T(8,128)(2,1)}), bf16[32,4,1024]{2,0,1:T(8,128)(2,1)}, u32[]{:S(2)}, u32[]{:S(2)}) async-start(bf16[32,4,1024]{2,0,1:T(8,128)(2,1)} %copy.89), calls=%async_computation | async-start | bytes 524288 | tf_op jit(solution)/shard_map/all_to_all | solution.py:115
  47.2 1.6 fusion.37
  48.8 6.5 %collective-permute-start.5 = (bf16[128,1024]{1,0:T(8,128)(2,1)}, bf16[128,1024]{1,0:T(8,128)(2,1)S(1)}, u32[]{:S(2)}, u32[]{:S(2)}) collective-permute-start(bf16[128,1024]{1,0:T(8,128)(2,1)} %bitcast.6), channel_id=1, source_target_pairs={{0,128},{1,129},{2,130},{3,131},{4,132},{5,133},{6,134},{7,135},{8... | collective-permute-start | bytes 786440 | tf_op jit(solution)/shard_map/ppermute | solution.py:37
  57.2 3.0 collective-permute-done.5
  60.2 26.3 %all-gather.2.cloned.1.call-done = bf16[1024,3072]{1,0:T(8,128)(2,1)} async-done(((bf16[32,3072]{1,0:T(8,128)(2,1)}), bf16[1024,3072]{1,0:T(8,128)(2,1)}) %all-gather.2.cloned.1.call-update) | async-done | bytes 6291472 | tf_op jit(solution)/shard_map/all_gather | solution.py:118
  86.5 3.2 fusion.12
  89.7 4.5 %all-to-all-start.1 = ((f32[4,32,1024]{2,1,0:T(8,128)}), f32[4,32,1024]{2,1,0:T(8,128)}, u32[]{:S(2)}, u32[]{:S(2)}) async-start(f32[4,32,1024]{2,1,0:T(8,128)} %bitcast.8), calls=%async_computation.1 | async-start | bytes 1048576 | tf_op jit(solution)/shard_map/all_to_all | solution.py:47
  95.8 6.4 %all-to-all-done.1 = f32[4,32,1024]{2,1,0:T(8,128)} async-done(((f32[4,32,1024]{2,1,0:T(8,128)}), f32[4,32,1024]{2,1,0:T(8,128)}, u32[]{:S(2)}, u32[]{:S(2)}) %all-to-all-start.1) | async-done | bytes 524320 | tf_op jit(solution)/shard_map/all_to_all | solution.py:47
  104.3 5.4 %all-to-all-start.2 = ((bf16[4,32,1024]{2,1,0:T(8,128)(2,1)}), bf16[4,32,1024]{2,1,0:T(8,128)(2,1)S(1)}, u32[]{:S(2)}, u32[]{:S(2)}) async-start(bf16[4,32,1024]{2,1,0:T(8,128)(2,1)} %broadcast_in_dim.20), calls=%async_computation.2 | async-start | bytes 524288 | tf_op jit(solution)/shard_map/all_to_all | solution.py:59
  110.1 2.8 collective-permute-start.4
  112.9 1.4 all-to-all-done.2
  114.3 2.1 fusion.6
  116.5 3.4 fusion.2
  119.9 6.2 %all-to-all-start.3 = ((f32[4,32,1024]{2,1,0:T(8,128)}), f32[4,32,1024]{2,1,0:T(8,128)}, u32[]{:S(2)}, u32[]{:S(2)}) async-start(f32[4,32,1024]{2,1,0:T(8,128)} %bitcast.10), calls=%async_computation.3 | async-start | bytes 1048576 | tf_op jit(solution)/shard_map/all_to_all | solution.py:47
  126.8 2.6 reshape.74
  129.4 1.9 copy.90
  131.3 3.8 all_to_all.56
  135.9 4.9 %all-to-all-start.5 = ((bf16[32,4,1024]{2,0,1:T(8,128)(2,1)}), bf16[32,4,1024]{2,0,1:T(8,128)(2,1)S(1)}, u32[]{:S(2)}, u32[]{:S(2)}) async-start(bf16[32,4,1024]{2,0,1:T(8,128)(2,1)} %copy.91), calls=%async_computation.5 | async-start | bytes 524288 | tf_op jit(solution)/shard_map/all_to_all | solution.py:123
  141.9 3.5 all-to-all-done.5
  145.4 9.1 %all_to_all.72 = bf16[4,32,1024]{2,1,0:T(8,128)(2,1)S(1)} all-to-all(bf16[4,32,1024]{2,1,0:T(8,128)(2,1)S(1)} %broadcast_in_dim.21), channel_id=1, replica_groups=mesh['role'=2,'dp'=32,'mp'=4] {'mp'}, dimensions={0} | all-to-all | bytes 524288 | tf_op jit(solution)/shard_map/all_to_all | solution.py:59
  154.5 2.1 fusion.97
  156.6 2.5 fusion.8
  159.2 10.6 %all_to_all.73 = f32[4,32,1024]{2,1,0:T(8,128)S(1)} all-to-all(f32[4,32,1024]{2,1,0:T(8,128)S(1)} %bitcast.82), channel_id=1, replica_groups=mesh['role'=2,'dp'=32,'mp'=4] {'mp'}, dimensions={0} | all-to-all | bytes 1048576 | tf_op jit(solution)/shard_map/all_to_all | solution.py:47
  169.9 9.0 %all_to_all.74 = bf16[4,32,1024]{2,1,0:T(8,128)(2,1)S(1)} all-to-all(bf16[4,32,1024]{2,1,0:T(8,128)(2,1)S(1)} %broadcast_in_dim.22), channel_id=1, replica_groups=mesh['role'=2,'dp'=32,'mp'=4] {'mp'}, dimensions={0} | all-to-all | bytes 524288 | tf_op jit(solution)/shard_map/all_to_all | solution.py:59
  178.9 2.3 fusion.17
  181.2 3.2 fusion.4
  184.4 5.5 %all-to-all-start.8 = ((f32[4,32,1024]{2,1,0:T(8,128)}), f32[4,32,1024]{2,1,0:T(8,128)S(1)}, u32[]{:S(2)}, u32[]{:S(2)}) async-start(f32[4,32,1024]{2,1,0:T(8,128)} %bitcast.81), calls=%async_computation.8 | async-start | bytes 1048576 | tf_op jit(solution)/shard_map/all_to_all | solution.py:47
  189.9 3.7 fusion.121
  193.6 2.8 fusion.112
  197.4 5.0 %all-to-all-start.9 = ((bf16[4,32,1024]{2,1,0:T(8,128)(2,1)}), bf16[4,32,1024]{2,1,0:T(8,128)(2,1)S(1)}, u32[]{:S(2)}, u32[]{:S(2)}) async-start(bf16[4,32,1024]{2,1,0:T(8,128)(2,1)} %broadcast_in_dim.23), calls=%async_computation.9 | async-start | bytes 524288 | tf_op jit(solution)/shard_map/all_to_all | solution.py:59
  202.4 2.8 fusion.122
  205.1 1.8 all-to-all-done.9
  207.0 3.1 convolution_add_fusion
  210.4 1.3 copy-done.1
  211.7 5.6 %pad_maximum_fusion = f32[1024,3072]{0,1:T(8,128)} fusion(f32[1024,1024]{0,1:T(8,128)S(1)} %copy-done, f32[1024,1024]{0,1:T(8,128)S(1)} %copy-done.1, f32[1024,1024]{0,1:T(8,128)S(1)} %convolution_add_fusion), kind=kLoop, calls=%fused_computation | loop fusion | flops 6291456 | bytes 25165824 | tf_op jit(solution)/shard_map/concatenate | solution.py:168
  217.3 12.6 %copy.99 = f32[1024,3072]{1,0:T(8,128)} copy(f32[1024,3072]{0,1:T(8,128)} %pad_maximum_fusion) | data formatting | bytes 25165824
  230.0 183.8 %reduce-scatter.4.cloned.1.call-done = f32[32,3072]{1,0:T(8,128)} async-done(((f32[1024,3072]{1,0:T(8,128)}), f32[32,3072]{1,0:T(8,128)}) %reduce-scatter.4.cloned.1.call-update) | async-done | bytes 393232 | tf_op jit(solution)/shard_map/reduce_scatter | solution.py:167
  413.8 1.3 collective-permute-start.6
  418.7 9.7 %collective-permute-done.6 = f32[32,3072]{1,0:T(8,128)} collective-permute-done((f32[32,3072]{1,0:T(8,128)}, f32[32,3072]{1,0:T(8,128)}, u32[]{:S(2)}, u32[]{:S(2)}) %collective-permute-start.6) | collective-permute-done | bytes 393248 | tf_op jit(solution)/shard_map/ppermute | solution.py:37
  428.3 1.5 copy.93
  (109 shorter events, 28.3 us)
Async XLA Ops:
  7.2 2.5 copy-start.3
  7.2 79.3 %all-gather.2.cloned.1.call-start = ((), (), s32[]{:S(2)}) async-start(), calls=%async_computation.11 | async-start | bytes 6488064 | tf_op jit(solution)/shard_map/all_gather | solution.py:118
  10.1 7.9 %collective-permute-start.1 = (f32[2,8,4,128]{3,1,2,0:T(8,128)S(1)}, f32[2,8,4,128]{3,1,2,0:T(8,128)S(1)}, u32[]{:S(2)}, u32[]{:S(2)}) collective-permute-start(f32[2,8,4,128]{3,1,2,0:T(8,128)S(1)} %get-tuple-element.66), channel_id=1, source_target_pairs={{4,0},{8,4},{12,8},{16,12},{20,16},{24,20},{28,24},{32,28},{36,32}... | collective-permute-start | bytes 98312 | tf_op jit(solution)/shard_map/ppermute | solution.py:27
  16.4 7.2 %collective-permute-start = (f32[2,8,4,128]{3,1,2,0:T(8,128)S(1)}, f32[2,8,4,128]{3,1,2,0:T(8,128)S(1)}, u32[]{:S(2)}, u32[]{:S(2)}) collective-permute-start(f32[2,8,4,128]{3,1,2,0:T(8,128)S(1)} %get-tuple-element.65), channel_id=1, source_target_pairs={{0,4},{4,8},{8,12},{12,16},{16,20},{20,24},{24,28},{28,32},{32,36}... | collective-permute-start | bytes 98312 | tf_op jit(solution)/shard_map/ppermute | solution.py:25
  24.1 16.0 %collective-permute-start.3 = (f32[2,8,72,4]{2,1,3,0:T(8,128)S(1)}, f32[2,8,72,4]{2,1,3,0:T(8,128)S(1)}, u32[]{:S(2)}, u32[]{:S(2)}) collective-permute-start(f32[2,8,72,4]{2,1,3,0:T(8,128)S(1)} %copy.81), channel_id=1, source_target_pairs={{1,0},{2,1},{3,2},{0,3},{5,4},{6,5},{7,6},{4,7},{9,8},{10,9},{11,1... | collective-permute-start | bytes 55304 | tf_op jit(solution)/shard_map/ppermute | solution.py:27
  25.2 15.2 %collective-permute-start.2 = (f32[2,8,72,4]{2,1,3,0:T(8,128)S(1)}, f32[2,8,72,4]{2,1,3,0:T(8,128)S(1)}, u32[]{:S(2)}, u32[]{:S(2)}) collective-permute-start(f32[2,8,72,4]{2,1,3,0:T(8,128)S(1)} %copy.80), channel_id=1, source_target_pairs={{0,1},{1,2},{2,3},{3,0},{4,5},{5,6},{6,7},{7,4},{8,9},{9,10},{10,1... | collective-permute-start | bytes 55304 | tf_op jit(solution)/shard_map/ppermute | solution.py:25
  35.6 13.2 %all-to-all-start = ((bf16[32,4,1024]{2,0,1:T(8,128)(2,1)}), bf16[32,4,1024]{2,0,1:T(8,128)(2,1)}, u32[]{:S(2)}, u32[]{:S(2)}) async-start(bf16[32,4,1024]{2,0,1:T(8,128)(2,1)} %copy.89), calls=%async_computation | async-start | bytes 524288 | tf_op jit(solution)/shard_map/all_to_all | solution.py:115
  48.8 7.2 %copy-start.2 = (f32[2,7,66,130]{3,1,2,0:T(8,128)S(1)}, f32[2,7,66,130]{3,1,2,0:T(8,128)}, u32[]{:S(2)}) copy-start(f32[2,7,66,130]{3,1,2,0:T(8,128)} %get-tuple-element.58) | copy-start | bytes 1441444
  48.8 11.4 %collective-permute-start.5 = (bf16[128,1024]{1,0:T(8,128)(2,1)}, bf16[128,1024]{1,0:T(8,128)(2,1)S(1)}, u32[]{:S(2)}, u32[]{:S(2)}) collective-permute-start(bf16[128,1024]{1,0:T(8,128)(2,1)} %bitcast.6), channel_id=1, source_target_pairs={{0,128},{1,129},{2,130},{3,131},{4,132},{5,133},{6,134},{7,135},{8... | collective-permute-start | bytes 786440 | tf_op jit(solution)/shard_map/ppermute | solution.py:37
  60.2 29.5 %copy-start.12 = (bf16[128,1024]{1,0:T(8,128)(2,1)}, bf16[128,1024]{1,0:T(8,128)(2,1)S(1)}, u32[]{:S(2)}) copy-start(bf16[128,1024]{1,0:T(8,128)(2,1)S(1)} %collective-permute-done.5) | copy-start | bytes 786436
  89.7 12.5 %all-to-all-start.1 = ((f32[4,32,1024]{2,1,0:T(8,128)}), f32[4,32,1024]{2,1,0:T(8,128)}, u32[]{:S(2)}, u32[]{:S(2)}) async-start(f32[4,32,1024]{2,1,0:T(8,128)} %bitcast.8), calls=%async_computation.1 | async-start | bytes 1048576 | tf_op jit(solution)/shard_map/all_to_all | solution.py:47
  104.3 10.1 %all-to-all-start.2 = ((bf16[4,32,1024]{2,1,0:T(8,128)(2,1)}), bf16[4,32,1024]{2,1,0:T(8,128)(2,1)S(1)}, u32[]{:S(2)}, u32[]{:S(2)}) async-start(bf16[4,32,1024]{2,1,0:T(8,128)(2,1)} %broadcast_in_dim.20), calls=%async_computation.2 | async-start | bytes 524288 | tf_op jit(solution)/shard_map/all_to_all | solution.py:59
  110.1 16.0 %collective-permute-start.4 = (f32[2,8,64,128]{3,2,1,0:T(8,128)S(1)}, f32[2,8,64,128]{3,2,1,0:T(8,128)S(1)}, u32[]{:S(2)}, u32[]{:S(2)}) collective-permute-start(f32[2,8,64,128]{3,2,1,0:T(8,128)S(1)} %copy.84), channel_id=1, source_target_pairs={{0,128},{1,129},{2,130},{3,131},{4,132},{5,133},{6,134},{7,135},{8... | collective-permute-start | bytes 1572872 | tf_op jit(solution)/shard_map/ppermute | solution.py:37
  114.3 2.1 copy-start.5
  116.5 3.4 copy-start.8
  119.9 16.0 %all-to-all-start.3 = ((f32[4,32,1024]{2,1,0:T(8,128)}), f32[4,32,1024]{2,1,0:T(8,128)}, u32[]{:S(2)}, u32[]{:S(2)}) async-start(f32[4,32,1024]{2,1,0:T(8,128)} %bitcast.10), calls=%async_computation.3 | async-start | bytes 1048576 | tf_op jit(solution)/shard_map/all_to_all | solution.py:47
  135.9 18.6 %copy-start.13 = (bf16[128,1024]{1,0:T(8,128)(2,1)S(1)}, bf16[128,1024]{1,0:T(8,128)(2,1)}, u32[]{:S(2)}) copy-start(bf16[128,1024]{1,0:T(8,128)(2,1)} %copy-done.12) | copy-start | bytes 786436
  135.9 9.5 %all-to-all-start.5 = ((bf16[32,4,1024]{2,0,1:T(8,128)(2,1)}), bf16[32,4,1024]{2,0,1:T(8,128)(2,1)S(1)}, u32[]{:S(2)}, u32[]{:S(2)}) async-start(bf16[32,4,1024]{2,0,1:T(8,128)(2,1)} %copy.91), calls=%async_computation.5 | async-start | bytes 524288 | tf_op jit(solution)/shard_map/all_to_all | solution.py:123
  156.6 2.5 copy-start.15
  159.1 19.8 %copy-start.9 = (f32[128,1024]{1,0:T(8,128)S(1)}, f32[128,1024]{1,0:T(8,128)}, u32[]{:S(2)}) copy-start(f32[128,1024]{1,0:T(8,128)} %copy-done.8) | copy-start | bytes 1572868
  184.4 12.0 %all-to-all-start.8 = ((f32[4,32,1024]{2,1,0:T(8,128)}), f32[4,32,1024]{2,1,0:T(8,128)S(1)}, u32[]{:S(2)}, u32[]{:S(2)}) async-start(f32[4,32,1024]{2,1,0:T(8,128)} %bitcast.81), calls=%async_computation.8 | async-start | bytes 1048576 | tf_op jit(solution)/shard_map/all_to_all | solution.py:47
  196.4 6.0 %copy-start.6 = (bf16[4,32,1024]{2,1,0:T(8,128)(2,1)S(1)}, bf16[4,32,1024]{2,1,0:T(8,128)(2,1)}, u32[]{:S(2)}) copy-start(bf16[4,32,1024]{2,1,0:T(8,128)(2,1)} %copy-done.5) | copy-start | bytes 786436
  197.4 9.6 %all-to-all-start.9 = ((bf16[4,32,1024]{2,1,0:T(8,128)(2,1)}), bf16[4,32,1024]{2,1,0:T(8,128)(2,1)S(1)}, u32[]{:S(2)}, u32[]{:S(2)}) async-start(bf16[4,32,1024]{2,1,0:T(8,128)(2,1)} %broadcast_in_dim.23), calls=%async_computation.9 | async-start | bytes 524288 | tf_op jit(solution)/shard_map/all_to_all | solution.py:59
  202.4 4.6 %copy-start.14 = (bf16[128,1024]{1,0:T(8,128)(2,1)S(1)}, bf16[128,1024]{1,0:T(8,128)(2,1)}, u32[]{:S(2)}) copy-start(bf16[128,1024]{1,0:T(8,128)(2,1)} %copy-done.12) | copy-start | bytes 786436
  202.4 211.5 %reduce-scatter.4.cloned.1.call-start = ((), (), s32[]{:S(2)}) async-start(), calls=%async_computation.12 | async-start | bytes 12976128 | tf_op jit(solution)/shard_map/reduce_scatter | solution.py:167
  207.0 3.5 copy-start
  207.0 4.7 %copy-start.1 = (f32[1024,1024]{0,1:T(8,128)S(1)}, f32[1024,1024]{0,1:T(8,128)}, u32[]{:S(2)}) copy-start(f32[1024,1024]{0,1:T(8,128)} %fusion.122) | copy-start | bytes 12582916
  230.0 185.1 %copy-start.16 = (bf16[1,32,1024]{2,1,0:T(8,128)(2,1)S(1)}, bf16[1,32,1024]{2,1,0:T(8,128)(2,1)}, u32[]{:S(2)}) copy-start(bf16[1,32,1024]{2,1,0:T(8,128)(2,1)} %param.6) | copy-start | bytes 196612
  230.0 186.0 %copy-start.18 = (f32[1,32,1024]{2,1,0:T(8,128)S(1)}, f32[1,32,1024]{2,1,0:T(8,128)}, u32[]{:S(2)}) copy-start(f32[1,32,1024]{2,1,0:T(8,128)} %param.8) | copy-start | bytes 393220
  413.8 14.5 %collective-permute-start.6 = (f32[32,3072]{1,0:T(8,128)}, f32[32,3072]{1,0:T(8,128)}, u32[]{:S(2)}, u32[]{:S(2)}) collective-permute-start(f32[32,3072]{1,0:T(8,128)} %reduce-scatter.4.cloned.1.call-done), channel_id=1, source_target_pairs={{128,0},{129,1},{130,2},{131,3},{132,4},{133,5},{134,6},{135,7},{1... | collective-permute-start | bytes 1179656 | tf_op jit(solution)/shard_map/ppermute | solution.py:37
  417.0 1.2 copy-start.11
  430.0 1.0 copy-start.4
  430.0 1.1 copy-start.7
  431.2 2.0 copy-start.10
  431.2 2.0 copy-start.17
Sparse Core Ops, SparseCore 0:
  10.4 76.0 all-gather.1
  230.1 183.6 reduce-scatter.3
where the time goes:
time: 442 us; the launch traced here: 441 us
  waiting for transfers between devices  243 us (55%)
  starting transfers between devices  56.4 us (13%)
  local copies, waits for them, and re-layouts  44.3 us (10%)
  matrix products  31.1 us (7%)
  blocking collectives  28.7 us (6%)
  other arithmetic  22.5 us (5%)
  between operations  14.5 us (3%)
    reduce_scatter x1, waiting for transfers between devices, shards(): lax.psum_scatter(jnp.concatenate([first + jnp.dot(embed_sent.T, initial_r...  184 us
    all_gather x1, waiting for transfers between devices, shards(): whole = lax.all_gather(stacked, 'dp', axis=0, tiled=True)  26.3 us
    unnamed x46, local copies, waits for them, and re-layouts  20.4 us
    all_to_all x2, blocking collectives, copy_for_each(): return lax.all_to_all(copies, axis, split_axis=0, concat_axis=0, tiled=True)  18.1 us
    all_to_all x3, starting transfers between devices, summed_on_arrival(): tiles = lax.all_to_all(in_blocks(x, dim, count), axis, 0, 0, tiled=True)  16.2 us
    ppermute x3, waiting for transfers between devices, from_behind(): lax.ppermute(value, axis, [(source, source + steps) for source in range(l...  12.7 us
    all_to_all x1, blocking collectives, summed_on_arrival(): tiles = lax.all_to_all(in_blocks(x, dim, count), axis, 0, 0, tiled=True)  10.6 us
    ppermute x3, starting transfers between devices, from_behind(): lax.ppermute(value, axis, [(source, source + steps) for source in range(l...  10.6 us
  transfers between devices with their start and end apart: 16, of which 10 were waited for; matrix products, arithmetic and copies ran while one was open for 10% of the time, Pallas kernels for 0%

commit v1 on v0

--- a/solution.py
+++ b/solution.py
@@ -115,7 +115,9 @@
     arranged = lax.all_to_all(to_patches(start_half), "mp", split_axis=1, concat_axis=0, tiled=True)
     initial_rows = from_behind(arranged, "role", 1)
     stacked = jnp.concatenate([embed[0], mlp[0, 0], mlp[0, 1]], axis=1)
-    whole = lax.all_gather(stacked, "dp", axis=0, tiled=True)
+    whole = jnp.concatenate(
+        lax.all_to_all(jnp.stack([stacked] * lax.axis_size("dp")), "dp", 0, 0), axis=0
+    )
     cells = advance(start_cells)
     arrived = from_behind(cells, "role", 1)
     state_out = jnp.where(group_index == 0, cells, arrived)

time: 442 us -> 560 us (1.27)
  waiting for transfers between devices: 243 us -> 348 us
  starting transfers between devices: 56.4 us -> 67.9 us
    ppermute x2, waiting for transfers between devices: 1.6 us -> 99.8 us  [extended(): lax.ppermute(head, axis, [((i + 1) % count, i) for i in range(count)])]
    all_gather x1 -> x0, waiting for transfers between devices: 26.3 us -> none  [shards(): whole = lax.all_gather(stacked, 'dp', axis=0, tiled=True)]
    reduce_scatter x1, waiting for transfers between devices: 184 us -> 203 us  [shards(): lax.psum_scatter(jnp.concatenate([first + jnp.dot(embed_sent.T, initial_r...]
    all_to_all x0 -> x1, waiting for transfers between devices: none -> 13.6 us  [shards(): lax.all_to_all(jnp.stack([stacked] * lax.axis_size('dp')), 'dp', 0, 0)]
    all_to_all x0 -> x1, starting transfers between devices: none -> 7.75 us  [shards(): lax.all_to_all(jnp.stack([stacked] * lax.axis_size('dp')), 'dp', 0, 0)]
    unnamed x46 -> x40, local copies, waits for them, and re-layouts: 20.4 us -> 20.4 us
  transfers between devices with their start and end apart: 16 -> 16, of which waited for: 10 -> 12; matrix products, arithmetic and copies ran while one was open for 10% -> 7% of each run, Pallas kernels for 0% -> 0%
where the time goes in v1:
time: 560 us; the launch traced here: 558 us
  waiting for transfers between devices  348 us (62%)
  starting transfers between devices  67.9 us (12%)
  local copies, waits for them, and re-layouts  46.8 us (8%)
  matrix products  31.2 us (6%)
  blocking collectives  28.9 us (5%)
  other arithmetic  21 us (4%)
  between operations  14.5 us (3%)
    reduce_scatter x1, waiting for transfers between devices, shards(): lax.psum_scatter(jnp.concatenate([first + jnp.dot(embed_sent.T, initial_r...  203 us
    ppermute x2, waiting for transfers between devices, extended(): lax.ppermute(head, axis, [((i + 1) % count, i) for i in range(count)])  99.8 us
    unnamed x40, local copies, waits for them, and re-layouts  20.4 us
    all_to_all x2, blocking collectives, copy_for_each(): return lax.all_to_all(copies, axis, split_axis=0, concat_axis=0, tiled=True)  18.1 us
    all_to_all x3, starting transfers between devices, summed_on_arrival(): tiles = lax.all_to_all(in_blocks(x, dim, count), axis, 0, 0, tiled=True)  17.9 us
    all_to_all x1, waiting for transfers between devices, shards(): lax.all_to_all(jnp.stack([stacked] * lax.axis_size('dp')), 'dp', 0, 0)  13.6 us
    ppermute x3, starting transfers between devices, from_behind(): lax.ppermute(value, axis, [(source, source + steps) for source in range(l...  12 us
  transfers between devices with their start and end apart: 16, of which 12 were waited for; matrix products, arithmetic and copies ran while one was open for 7% of the time, Pallas kernels for 0%

profile of v1, /device:TPU:24, one launch (start us, length us, event | category | flops | bytes accessed | tf_op | source)
XLA Modules:
  0.0 558.1 jit_solution(16478340711368141383)
XLA Ops:
  8.3 1.4 convert_element_type.57
  9.6 1.9 copy.104
  11.5 3.8 all_to_all.52
  16.1 5.9 %all-to-all-start.1 = ((bf16[32,4,1024]{2,0,1:T(8,128)(2,1)}), bf16[32,4,1024]{2,0,1:T(8,128)(2,1)}, u32[]{:S(2)}, u32[]{:S(2)}) async-start(bf16[32,4,1024]{2,0,1:T(8,128)(2,1)} %copy.89), calls=%async_computation.1 | async-start | bytes 524288 | tf_op jit(solution)/shard_map/all_to_all | solution.py:115
  22.1 4.7 all-to-all-done.1
  26.8 3.4 stack.20
  30.2 7.8 %all-to-all-start = ((bf16[32,32,3072]{2,1,0:T(8,128)(2,1)}), bf16[32,32,3072]{2,1,0:T(8,128)(2,1)}, u32[]{:S(2)}, u32[]{:S(2)}) async-start(bf16[32,32,3072]{2,1,0:T(8,128)(2,1)} %stack.20), calls=%async_computation | async-start | bytes 12582912 | tf_op jit(solution)/shard_map/all_to_all | solution.py:119
  38.3 5.5 collective-permute-start.1
  43.8 98.4 %collective-permute-done.1 = f32[2,8,4,128]{3,1,2,0:T(8,128)S(1)} collective-permute-done((f32[2,8,4,128]{3,1,2,0:T(8,128)S(1)}, f32[2,8,4,128]{3,1,2,0:T(8,128)S(1)}, u32[]{:S(2)}, u32[]{:S(2)}) %collective-permute-start.1) | collective-permute-done | bytes 32800 | tf_op jit(solution)/shard_map/ppermute | solution.py:27
  142.2 4.3 collective-permute-done
  147.4 3.4 collective-permute-start.2
  150.8 1.4 collective-permute-done.3
  160.0 7.1 %collective-permute-start.5 = (bf16[128,1024]{1,0:T(8,128)(2,1)}, bf16[128,1024]{1,0:T(8,128)(2,1)}, u32[]{:S(2)}, u32[]{:S(2)}) collective-permute-start(bf16[128,1024]{1,0:T(8,128)(2,1)} %bitcast.7), channel_id=1, source_target_pairs={{0,128},{1,129},{2,130},{3,131},{4,132},{5,133},{6,134},{7,135},{8... | collective-permute-start | bytes 786440 | tf_op jit(solution)/shard_map/ppermute | solution.py:37
  168.9 1.7 collective-permute-done.5
  170.6 13.6 %all-to-all-done = bf16[32,32,3072]{2,1,0:T(8,128)(2,1)} async-done(((bf16[32,32,3072]{2,1,0:T(8,128)(2,1)}), bf16[32,32,3072]{2,1,0:T(8,128)(2,1)}, u32[]{:S(2)}, u32[]{:S(2)}) %all-to-all-start) | async-done | bytes 6291488 | tf_op jit(solution)/shard_map/all_to_all | solution.py:119
  184.1 3.2 fusion.12
  187.4 6.2 %all-to-all-start.2 = ((f32[4,32,1024]{2,1,0:T(8,128)}), f32[4,32,1024]{2,1,0:T(8,128)}, u32[]{:S(2)}, u32[]{:S(2)}) async-start(f32[4,32,1024]{2,1,0:T(8,128)} %bitcast.9), calls=%async_computation.2 | async-start | bytes 1048576 | tf_op jit(solution)/shard_map/all_to_all | solution.py:47
  195.1 5.8 %all-to-all-done.2 = f32[4,32,1024]{2,1,0:T(8,128)} async-done(((f32[4,32,1024]{2,1,0:T(8,128)}), f32[4,32,1024]{2,1,0:T(8,128)}, u32[]{:S(2)}, u32[]{:S(2)}) %all-to-all-start.2) | async-done | bytes 524320 | tf_op jit(solution)/shard_map/all_to_all | solution.py:47
  202.9 5.4 all-to-all-start.3
  208.7 3.6 collective-permute-start.4
  213.0 2.1 fusion.6
  215.1 3.4 fusion.2
  218.5 6.2 %all-to-all-start.4 = ((f32[4,32,1024]{2,1,0:T(8,128)}), f32[4,32,1024]{2,1,0:T(8,128)}, u32[]{:S(2)}, u32[]{:S(2)}) async-start(f32[4,32,1024]{2,1,0:T(8,128)} %bitcast.11), calls=%async_computation.4 | async-start | bytes 1048576 | tf_op jit(solution)/shard_map/all_to_all | solution.py:47
  225.5 2.6 reshape.80
  228.0 1.9 copy.90
  230.0 3.8 all_to_all.60
  234.5 4.8 all-to-all-start.6
  240.4 3.5 all-to-all-done.6
  243.9 9.1 %all_to_all.77 = bf16[4,32,1024]{2,1,0:T(8,128)(2,1)S(1)} all-to-all(bf16[4,32,1024]{2,1,0:T(8,128)(2,1)S(1)} %broadcast_in_dim.21), channel_id=1, replica_groups=mesh['role'=2,'dp'=32,'mp'=4] {'mp'}, dimensions={0} | all-to-all | bytes 524288 | tf_op jit(solution)/shard_map/all_to_all | solution.py:59
  253.0 2.1 fusion.97
  255.1 2.5 fusion.8
  257.7 10.8 %all_to_all.78 = f32[4,32,1024]{2,1,0:T(8,128)S(1)} all-to-all(f32[4,32,1024]{2,1,0:T(8,128)S(1)} %bitcast.83), channel_id=1, replica_groups=mesh['role'=2,'dp'=32,'mp'=4] {'mp'}, dimensions={0} | all-to-all | bytes 1048576 | tf_op jit(solution)/shard_map/all_to_all | solution.py:47
  268.5 9.1 %all_to_all.79 = bf16[4,32,1024]{2,1,0:T(8,128)(2,1)S(1)} all-to-all(bf16[4,32,1024]{2,1,0:T(8,128)(2,1)S(1)} %broadcast_in_dim.22), channel_id=1, replica_groups=mesh['role'=2,'dp'=32,'mp'=4] {'mp'}, dimensions={0} | all-to-all | bytes 524288 | tf_op jit(solution)/shard_map/all_to_all | solution.py:59
  277.6 2.3 fusion.17
  279.8 3.2 fusion.4
  283.0 5.5 all-to-all-start.9
  288.5 3.7 fusion.121
  292.3 2.8 fusion.112
  296.0 5.1 all-to-all-start.10
  301.1 2.8 fusion.122
  303.9 1.8 all-to-all-done.10
  305.7 3.2 convolution_add_fusion
  310.5 5.6 %pad_maximum_fusion = f32[1024,3072]{0,1:T(8,128)} fusion(f32[1024,1024]{0,1:T(8,128)S(1)} %copy-done, f32[1024,1024]{0,1:T(8,128)S(1)} %copy-done.1, f32[1024,1024]{0,1:T(8,128)S(1)} %convolution_add_fusion), kind=kLoop, calls=%fused_computation | loop fusion | flops 6291456 | bytes 25165824 | tf_op jit(solution)/shard_map/concatenate | solution.py:170
  316.1 12.6 %copy.99 = f32[1024,3072]{1,0:T(8,128)} copy(f32[1024,3072]{0,1:T(8,128)} %pad_maximum_fusion) | data formatting | bytes 25165824
  328.8 202.8 %reduce-scatter.4.cloned.1.call-done = f32[32,3072]{1,0:T(8,128)} async-done(((f32[1024,3072]{1,0:T(8,128)}), f32[32,3072]{1,0:T(8,128)}) %reduce-scatter.4.cloned.1.call-update) | async-done | bytes 393232 | tf_op jit(solution)/shard_map/reduce_scatter | solution.py:169
  531.6 1.3 collective-permute-start.6
  536.5 9.1 %collective-permute-done.6 = f32[32,3072]{1,0:T(8,128)} collective-permute-done((f32[32,3072]{1,0:T(8,128)}, f32[32,3072]{1,0:T(8,128)}, u32[]{:S(2)}, u32[]{:S(2)}) %collective-permute-start.6) | collective-permute-done | bytes 393248 | tf_op jit(solution)/shard_map/ppermute | solution.py:37
  545.6 1.5 copy.93
  (103 shorter events, 30.1 us)
Async XLA Ops:
  11.5 10.5 %copy-start.9 = (bf16[1,2,32,1024]{3,2,1,0:T(8,128)(2,1)S(1)}, bf16[1,2,32,1024]{3,2,1,0:T(8,128)(2,1)}, u32[]{:S(2)}) copy-start(bf16[1,2,32,1024]{3,2,1,0:T(8,128)(2,1)} %param.7) | copy-start | bytes 393220
  15.3 6.7 %copy-start.12 = (bf16[1,32,1024]{2,1,0:T(8,128)(2,1)S(1)}, bf16[1,32,1024]{2,1,0:T(8,128)(2,1)}, u32[]{:S(2)}) copy-start(bf16[1,32,1024]{2,1,0:T(8,128)(2,1)} %param.6) | copy-start | bytes 196612
  16.1 10.6 %all-to-all-start.1 = ((bf16[32,4,1024]{2,0,1:T(8,128)(2,1)}), bf16[32,4,1024]{2,0,1:T(8,128)(2,1)}, u32[]{:S(2)}, u32[]{:S(2)}) async-start(bf16[32,4,1024]{2,0,1:T(8,128)(2,1)} %copy.89), calls=%async_computation.1 | async-start | bytes 524288 | tf_op jit(solution)/shard_map/all_to_all | solution.py:115
  30.2 7.8 %copy-start.2 = (f32[1,2,8,64,128]{4,3,2,1,0:T(8,128)S(1)}, f32[1,2,8,64,128]{4,3,2,1,0:T(8,128)}, u32[]{:S(2)}) copy-start(f32[1,2,8,64,128]{4,3,2,1,0:T(8,128)} %param.5) | copy-start | bytes 1572868
  30.2 154.0 %all-to-all-start = ((bf16[32,32,3072]{2,1,0:T(8,128)(2,1)}), bf16[32,32,3072]{2,1,0:T(8,128)(2,1)}, u32[]{:S(2)}, u32[]{:S(2)}) async-start(bf16[32,32,3072]{2,1,0:T(8,128)(2,1)} %stack.20), calls=%async_computation | async-start | bytes 12582912 | tf_op jit(solution)/shard_map/all_to_all | solution.py:119
  38.3 103.9 %collective-permute-start.1 = (f32[2,8,4,128]{3,1,2,0:T(8,128)S(1)}, f32[2,8,4,128]{3,1,2,0:T(8,128)S(1)}, u32[]{:S(2)}, u32[]{:S(2)}) collective-permute-start(f32[2,8,4,128]{3,1,2,0:T(8,128)S(1)} %get-tuple-element.66), channel_id=1, source_target_pairs={{4,0},{8,4},{12,8},{16,12},{20,16},{24,20},{28,24},{32,28},{36,32}... | collective-permute-start | bytes 98312 | tf_op jit(solution)/shard_map/ppermute | solution.py:27
  43.8 102.7 %collective-permute-start = (f32[2,8,4,128]{3,1,2,0:T(8,128)S(1)}, f32[2,8,4,128]{3,1,2,0:T(8,128)S(1)}, u32[]{:S(2)}, u32[]{:S(2)}) collective-permute-start(f32[2,8,4,128]{3,1,2,0:T(8,128)S(1)} %get-tuple-element.65), channel_id=1, source_target_pairs={{0,4},{4,8},{8,12},{12,16},{16,20},{20,24},{24,28},{28,32},{32,36}... | collective-permute-start | bytes 98312 | tf_op jit(solution)/shard_map/ppermute | solution.py:25
  147.1 5.2 collective-permute-start.3
  147.4 5.2 collective-permute-start.2
  160.0 10.6 %collective-permute-start.5 = (bf16[128,1024]{1,0:T(8,128)(2,1)}, bf16[128,1024]{1,0:T(8,128)(2,1)}, u32[]{:S(2)}, u32[]{:S(2)}) collective-permute-start(bf16[128,1024]{1,0:T(8,128)(2,1)} %bitcast.7), channel_id=1, source_target_pairs={{0,128},{1,129},{2,130},{3,131},{4,132},{5,133},{6,134},{7,135},{8... | collective-permute-start | bytes 786440 | tf_op jit(solution)/shard_map/ppermute | solution.py:37
  187.4 13.5 %all-to-all-start.2 = ((f32[4,32,1024]{2,1,0:T(8,128)}), f32[4,32,1024]{2,1,0:T(8,128)}, u32[]{:S(2)}, u32[]{:S(2)}) async-start(f32[4,32,1024]{2,1,0:T(8,128)} %bitcast.9), calls=%async_computation.2 | async-start | bytes 1048576 | tf_op jit(solution)/shard_map/all_to_all | solution.py:47
  202.9 10.1 %all-to-all-start.3 = ((bf16[4,32,1024]{2,1,0:T(8,128)(2,1)}), bf16[4,32,1024]{2,1,0:T(8,128)(2,1)S(1)}, u32[]{:S(2)}, u32[]{:S(2)}) async-start(bf16[4,32,1024]{2,1,0:T(8,128)(2,1)} %broadcast_in_dim.20), calls=%async_computation.3 | async-start | bytes 524288 | tf_op jit(solution)/shard_map/all_to_all | solution.py:59
  208.7 16.0 %collective-permute-start.4 = (f32[2,8,64,128]{3,2,1,0:T(8,128)S(1)}, f32[2,8,64,128]{3,2,1,0:T(8,128)S(1)}, u32[]{:S(2)}, u32[]{:S(2)}) collective-permute-start(f32[2,8,64,128]{3,2,1,0:T(8,128)S(1)} %copy.84), channel_id=1, source_target_pairs={{0,128},{1,129},{2,130},{3,131},{4,132},{5,133},{6,134},{7,135},{8... | collective-permute-start | bytes 1572872 | tf_op jit(solution)/shard_map/ppermute | solution.py:37
  213.0 2.1 copy-start.4
  215.1 3.4 copy-start.7
  218.5 16.0 %all-to-all-start.4 = ((f32[4,32,1024]{2,1,0:T(8,128)}), f32[4,32,1024]{2,1,0:T(8,128)}, u32[]{:S(2)}, u32[]{:S(2)}) async-start(f32[4,32,1024]{2,1,0:T(8,128)} %bitcast.11), calls=%async_computation.4 | async-start | bytes 1048576 | tf_op jit(solution)/shard_map/all_to_all | solution.py:47
  234.5 9.4 %all-to-all-start.6 = ((bf16[32,4,1024]{2,0,1:T(8,128)(2,1)}), bf16[32,4,1024]{2,0,1:T(8,128)(2,1)S(1)}, u32[]{:S(2)}, u32[]{:S(2)}) async-start(bf16[32,4,1024]{2,0,1:T(8,128)(2,1)} %copy.91), calls=%async_computation.6 | async-start | bytes 524288 | tf_op jit(solution)/shard_map/all_to_all | solution.py:125
  255.1 2.5 copy-start.11
  257.6 19.9 %copy-start.8 = (f32[128,1024]{1,0:T(8,128)S(1)}, f32[128,1024]{1,0:T(8,128)}, u32[]{:S(2)}) copy-start(f32[128,1024]{1,0:T(8,128)} %copy-done.7) | copy-start | bytes 1572868
  283.0 12.0 %all-to-all-start.9 = ((f32[4,32,1024]{2,1,0:T(8,128)}), f32[4,32,1024]{2,1,0:T(8,128)S(1)}, u32[]{:S(2)}, u32[]{:S(2)}) async-start(f32[4,32,1024]{2,1,0:T(8,128)} %bitcast.82), calls=%async_computation.9 | async-start | bytes 1048576 | tf_op jit(solution)/shard_map/all_to_all | solution.py:47
  295.0 6.1 %copy-start.5 = (bf16[4,32,1024]{2,1,0:T(8,128)(2,1)S(1)}, bf16[4,32,1024]{2,1,0:T(8,128)(2,1)}, u32[]{:S(2)}) copy-start(bf16[4,32,1024]{2,1,0:T(8,128)(2,1)} %copy-done.4) | copy-start | bytes 786436
  296.0 9.7 %all-to-all-start.10 = ((bf16[4,32,1024]{2,1,0:T(8,128)(2,1)}), bf16[4,32,1024]{2,1,0:T(8,128)(2,1)S(1)}, u32[]{:S(2)}, u32[]{:S(2)}) async-start(bf16[4,32,1024]{2,1,0:T(8,128)(2,1)} %broadcast_in_dim.23), calls=%async_computation.10 | async-start | bytes 524288 | tf_op jit(solution)/shard_map/all_to_all | solution.py:59
  301.1 230.5 %reduce-scatter.4.cloned.1.call-start = ((), (), s32[]{:S(2)}) async-start(), calls=%async_computation.12 | async-start | bytes 12976128 | tf_op jit(solution)/shard_map/reduce_scatter | solution.py:169
  305.7 3.5 copy-start
  305.7 4.8 copy-start.1
  328.8 204.2 %copy-start.13 = (bf16[1,32,1024]{2,1,0:T(8,128)(2,1)S(1)}, bf16[1,32,1024]{2,1,0:T(8,128)(2,1)}, u32[]{:S(2)}) copy-start(bf16[1,32,1024]{2,1,0:T(8,128)(2,1)} %param.6) | copy-start | bytes 196612
  328.8 205.0 %copy-start.15 = (f32[1,32,1024]{2,1,0:T(8,128)S(1)}, f32[1,32,1024]{2,1,0:T(8,128)}, u32[]{:S(2)}) copy-start(f32[1,32,1024]{2,1,0:T(8,128)} %param.8) | copy-start | bytes 393220
  531.6 14.0 %collective-permute-start.6 = (f32[32,3072]{1,0:T(8,128)}, f32[32,3072]{1,0:T(8,128)}, u32[]{:S(2)}, u32[]{:S(2)}) collective-permute-start(f32[32,3072]{1,0:T(8,128)} %reduce-scatter.4.cloned.1.call-done), channel_id=1, source_target_pairs={{128,0},{129,1},{130,2},{131,3},{132,4},{133,5},{134,6},{135,7},{1... | collective-permute-start | bytes 1179656 | tf_op jit(solution)/shard_map/ppermute | solution.py:37
  534.8 1.2 copy-start.10
  547.2 1.0 copy-start.3
  547.3 1.1 copy-start.6
  548.5 2.0 copy-start.14
Sparse Core Ops, SparseCore 0:
  328.9 202.6 reduce-scatter.3
